TPU v7x, 512 devices: a whole 4x4x16 slice. The times are simulated.
512 devices in a mesh: space: 16 (over z_hi, x), inst: 32 (over y, z_lo, core).
Axes of the slice: x: 4, y: 4, z: 16 (z_hi: 4, z_lo: 4; z = z_hi * 4 + z_lo), core: 2. Of those that a mesh axis runs over, the one named last changes fastest.
Arguments:
- flow_state: float32 [32, 7, 65536], P('inst', None, 'space'), may hold values from -5.5 to 5.5
- face_nbr: int32 [6, 65536], P(None, 'space'), may hold values from 0 to 5119
- halo_send: int32 [2, 8192], P(None, 'space'), may hold values from 0 to 4095, as said below
- face_area: float32 [3, 6, 65536], P(None, None, 'space'), may hold values from -3 to 3
- cell_volume: float32 [65536], P(('space', 'inst')), may hold values from 0.5 to 2
- flux_left: float32 [7, 7], replicated, may hold values from -2 to 2
- flux_right: float32 [7, 7], replicated, may hold values from -2 to 2
Outputs:
- inverse: float32 [2, 7, 7, 16, 65536], P(None, None, None, None, ('space', 'inst'))
Inputs may be any that keep to these rules, and one draw needn't show every extreme that they name: `halo_send`: within each slab's block of 512 columns, row 0 lists each cell of local indices (7) * 512 to 4095 once and row 1 each cell of local indices 0 to 511 once.
All inputs are finite; a program needn't handle non-finite values.
Results may differ from a plain program's by a relative error of at most 0.0001.
Values sent between devices are 32-bit elements; how exact they have to be, the bound alone decides.
A program may use at most 128 MiB of HBM per device.

v0:
```python
import jax
import jax.numpy as jnp
from jax import lax
from jax.sharding import PartitionSpec as P

INSTANCES = 32
HARM = 16
frequency = 0.1


def shifted(block, axis, distance):
    devices = range(lax.axis_size(axis))
    route = [(i - distance, i) for i in devices if i - distance in devices]
    return lax.ppermute(block, axis, route)


def face_jacobian(face_mean, normal_flux, flux_left, flux_right):
    coupling = flux_left[:, :, None] * flux_right[None, :, :]
    jacobian = jnp.einsum("imj,bmc->bijc", coupling, face_mean, precision=lax.Precision.HIGHEST)
    identity = jnp.eye(face_mean.shape[1], dtype=jnp.float32)
    jacobian = jacobian + normal_flux[:, None, None, :] * identity[None, :, :, None]
    spectral = jnp.max(jnp.sum(jnp.abs(jacobian), axis=2), axis=1) + 0.5
    return (jacobian, spectral, identity)


def face_terms(face_mean, normal_flux, flux_left, flux_right):
    jacobian, spectral, identity = face_jacobian(face_mean, normal_flux, flux_left, flux_right)
    return jnp.sum(
        0.5 * (jacobian + spectral[:, None, None, :] * identity[None, :, :, None]), axis=0
    )


def invert(real_part, imag_part):
    size_vars = real_part.shape[0]
    identity = jnp.broadcast_to(
        jnp.eye(size_vars, dtype=jnp.float32)[:, :, None, None], real_part.shape
    )
    aug_real = jnp.concatenate([real_part, identity], axis=1)
    aug_imag = jnp.concatenate([imag_part, jnp.zeros_like(identity)], axis=1)
    for column in range(size_vars):
        lead_real = aug_real[column, column]
        lead_imag = aug_imag[column, column]
        inverse_norm = 1.0 / (lead_real * lead_real + lead_imag * lead_imag)
        recip_real = lead_real * inverse_norm
        recip_imag = -lead_imag * inverse_norm
        row_real = aug_real[column] * recip_real - aug_imag[column] * recip_imag
        row_imag = aug_real[column] * recip_imag + aug_imag[column] * recip_real
        col_real = aug_real[:, column : column + 1]
        col_imag = aug_imag[:, column : column + 1]
        aug_real = aug_real - (col_real * row_real[None] - col_imag * row_imag[None])
        aug_imag = aug_imag - (col_real * row_imag[None] + col_imag * row_real[None])
        aug_real = aug_real.at[column].set(row_real)
        aug_imag = aug_imag.at[column].set(row_imag)
    return (aug_real[:, size_vars:], aug_imag[:, size_vars:])


def per_device(flow_state, face_nbr, halo_send, face_area, cell_volume, flux_left, flux_right):
    components = flow_state.shape[1]
    cell_count = flow_state.shape[2]
    face_count = face_nbr.shape[0]
    owners = lax.axis_size("inst")
    share_cells = cell_count // owners
    upward = flow_state[:, :, halo_send[0]]
    downward = flow_state[:, :, halo_send[1]]
    from_lower = shifted(upward, "space", 1)
    from_upper = shifted(downward, "space", -1)
    extended = jnp.concatenate([flow_state, from_lower, from_upper], axis=2)
    running = jnp.zeros((components, components, cell_count), jnp.float32)
    for direction in range(face_count):
        neighbour = jnp.take(extended, face_nbr[direction], axis=2)
        face_mean = 0.5 * (flow_state + neighbour)
        normals = face_area[:, direction]
        normal_flux = (
            face_mean[:, 1] * normals[0]
            + face_mean[:, 2] * normals[1]
            + face_mean[:, 3] * normals[2]
        )
        face_mean, normal_flux = (face_mean, normal_flux)
        running = running + face_terms(face_mean, normal_flux, flux_left, flux_right)
    everything = lax.psum(running, "inst")
    summed = lax.dynamic_slice_in_dim(
        everything, lax.axis_index("inst") * share_cells, share_cells, 2
    )
    jacobian_mean = summed / (face_count * INSTANCES)
    harmonics = jnp.arange(1, HARM + 1, dtype=jnp.int32).astype(jnp.float32)
    imag_shift = harmonics[:, None] * frequency * cell_volume[None, :]
    real_part = jnp.broadcast_to(
        jacobian_mean[:, :, None, :], (components, components, HARM, share_cells)
    )
    imag_part = jnp.eye(components, dtype=jnp.float32)[:, :, None, None] * imag_shift[None, None]
    inv_real, inv_imag = invert(real_part, imag_part)
    return jnp.stack([inv_real, inv_imag])


def solution(mesh):
    placed = (
        P("inst", None, "space"),
        P(None, "space"),
        P(None, "space"),
        P(None, None, "space"),
        P(("space", "inst")),
        P(),
        P(),
    )
    return jax.shard_map(
        per_device,
        mesh=mesh,
        in_specs=placed,
        out_specs=P(None, None, None, None, ("space", "inst")),
        check_vma=False,
    )
```

profile of v0, /device:TPU:2, one launch (start us, length us, event | category | flops | bytes accessed | tf_op | source)
XLA Modules:
  0.0 463.7 jit_solution(6853187282242230879)
XLA Ops:
  6.5 1.6 copy.196
  8.2 1.0 gather_fusion
  9.2 3.4 collective-permute-start
  12.7 1.0 gather_fusion.1
  13.7 5.7 %collective-permute-start.1 = (f32[1,7,512]{1,2,0:T(8,128)S(1)}, f32[1,7,512]{1,2,0:T(8,128)S(1)}, u32[]{:S(2)}, u32[]{:S(2)}) collective-permute-start(f32[1,7,512]{1,2,0:T(8,128)S(1)} %bitcast.361), channel_id=1, source_target_pairs={{32,0},{64,32},{96,64},{128,96},{160,128},{192,160},{224,192},{256... | collective-permute-start | bytes 43016 | tf_op jit(solution)/shard_map/ppermute | solution.py:14
  19.4 0.1 fusion.97
  19.5 0.6 compare_and_fusion
  20.2 0.6 compare_and_fusion.2
  20.8 0.6 compare_and_fusion.4
  21.4 0.1 copy.199
  21.5 1.9 collective-permute-done.1
  23.4 1.8 maximum_bitcast_fusion
  25.1 14.2 %gather_fusion.2 = f32[4096,7]{1,0:T(8,128)} fusion(f32[7,5120]{0,1:T(8,128)S(1)} %maximum_bitcast_fusion, s32[4096]{0:T(1024)S(1)} %fusion.74), kind=kCustom, calls=%fused_computation.clone | custom fusion | bytes 245760 | tf_op jit(solution)/shard_map/jit(_take)/gather | solution.py:70
  39.3 2.2 copy.197
  41.5 14.2 %gather_fusion.3 = f32[4096,7]{1,0:T(8,128)} fusion(f32[7,5120]{0,1:T(8,128)S(1)} %maximum_bitcast_fusion, s32[4096]{0:T(1024)S(1)} %fusion.75), kind=kCustom, calls=%fused_computation.1.clone | custom fusion | bytes 245760 | tf_op jit(solution)/shard_map/jit(_take)/gather | solution.py:70
  55.7 2.2 copy.200
  57.9 14.2 %gather_fusion.4 = f32[4096,7]{1,0:T(8,128)} fusion(f32[7,5120]{0,1:T(8,128)S(1)} %maximum_bitcast_fusion, s32[4096]{0:T(1024)S(1)} %fusion.76), kind=kCustom, calls=%fused_computation.2.clone | custom fusion | bytes 245760 | tf_op jit(solution)/shard_map/jit(_take)/gather | solution.py:70
  72.1 2.2 copy.202
  74.3 14.2 %gather_fusion.5 = f32[4096,7]{1,0:T(8,128)} fusion(f32[7,5120]{0,1:T(8,128)S(1)} %maximum_bitcast_fusion, s32[4096]{0:T(1024)S(1)} %fusion.77), kind=kCustom, calls=%fused_computation.3.clone | custom fusion | bytes 245760 | tf_op jit(solution)/shard_map/jit(_take)/gather | solution.py:70
  88.5 2.9 copy.204
  91.3 14.2 %gather_fusion.6 = f32[4096,7]{1,0:T(8,128)} fusion(f32[7,5120]{0,1:T(8,128)S(1)} %maximum_bitcast_fusion, s32[4096]{0:T(1024)S(1)} %fusion.78), kind=kCustom, calls=%fused_computation.4.clone | custom fusion | bytes 245760 | tf_op jit(solution)/shard_map/jit(_take)/gather | solution.py:70
  105.5 2.9 copy.206
  108.4 14.2 %gather_fusion.7 = f32[4096,7]{1,0:T(8,128)} fusion(f32[7,5120]{0,1:T(8,128)S(1)} %maximum_bitcast_fusion, s32[4096]{0:T(1024)S(1)} %fusion.79), kind=kCustom, calls=%fused_computation.5.clone | custom fusion | bytes 245760 | tf_op jit(solution)/shard_map/jit(_take)/gather | solution.py:70
  122.6 2.3 copy.208
  125.0 0.2 fusion.7
  125.2 1.6 fusion.36
  126.8 1.1 abs_reduce_fusion.5
  128.0 1.1 abs_reduce_fusion.4
  129.2 1.1 abs_reduce_fusion.3
  130.4 1.6 fusion.30
  132.1 2.1 abs_reduce_fusion.2
  134.2 2.1 abs_reduce_fusion.1
  136.3 2.1 abs_reduce_fusion
  138.5 3.3 multiply_bitcast_fusion
  141.8 0.0 all-reduce.3.cloned.1.call-update
  141.8 0.1 broadcast_multiply_fusion.1
  141.9 0.1 broadcast_multiply_fusion
  142.0 310.4 %all-reduce.3.cloned.1.call-done = f32[7,7,4096]{2,1,0:T(8,128)} async-done(((f32[7,7,4096]{2,1,0:T(8,128)}), f32[7,7,4096]{2,1,0:T(8,128)}) %all-reduce.3.cloned.1.call-update) | async-done | bytes 802832 | tf_op jit(solution)/shard_map/psum | solution.py:80
  452.5 0.8 dynamic-slice_multiply_fusion
  453.3 0.1 broadcast_in_dim.22
  453.5 0.2 fusion.6
  453.8 0.2 subtract_subtract_fusion.5
  454.2 0.2 subtract_subtract_fusion.4
  454.5 0.2 subtract_subtract_fusion.3
  454.9 0.2 subtract_subtract_fusion.2
  455.2 0.2 subtract_subtract_fusion.1
  455.6 0.2 subtract_subtract_fusion
  455.9 1.0 pad_maximum_fusion.1
  (94 shorter events, 1.1 us)
Async XLA Ops:
  6.5 1.6 copy-start.11
  6.5 12.9 %copy-start.5 = (s32[6,4096]{1,0:T(8,128)S(1)}, s32[6,4096]{1,0:T(8,128)}, u32[]{:S(2)}) copy-start(s32[6,4096]{1,0:T(8,128)} %param.38) | copy-start | bytes 294916
  6.5 14.9 %copy-start.12 = (f32[7,7]{1,0:T(8,128)S(1)}, f32[7,7]{1,0:T(8,128)}, u32[]{:S(2)}) copy-start(f32[7,7]{1,0:T(8,128)} %param.43) | copy-start | bytes 592
  6.5 445.9 %all-reduce.3.cloned.1.call-start = ((), (), s32[]{:S(2)}) async-start(), calls=%async_computation | async-start | bytes 1835008 | tf_op jit(solution)/shard_map/psum | solution.py:80
  8.1 13.4 %copy-start = (f32[1,7,4096]{1,2,0:T(8,128)}, f32[1,7,4096]{1,2,0:T(8,128)S(1)}, u32[]{:S(2)}) copy-start(f32[1,7,4096]{1,2,0:T(8,128)S(1)} %copy.196) | copy-start | bytes 344068
  9.2 12.3 %collective-permute-start = (f32[1,7,512]{1,2,0:T(8,128)S(1)}, f32[1,7,512]{1,2,0:T(8,128)S(1)}, u32[]{:S(2)}, u32[]{:S(2)}) collective-permute-start(f32[1,7,512]{1,2,0:T(8,128)S(1)} %bitcast.360), channel_id=1, source_target_pairs={{0,32},{32,64},{64,96},{96,128},{128,160},{160,192},{192,224},{224... | collective-permute-start | bytes 43016 | tf_op jit(solution)/shard_map/ppermute | solution.py:14
  13.7 9.7 %collective-permute-start.1 = (f32[1,7,512]{1,2,0:T(8,128)S(1)}, f32[1,7,512]{1,2,0:T(8,128)S(1)}, u32[]{:S(2)}, u32[]{:S(2)}) collective-permute-start(f32[1,7,512]{1,2,0:T(8,128)S(1)} %bitcast.361), channel_id=1, source_target_pairs={{32,0},{64,32},{96,64},{128,96},{160,128},{192,160},{224,192},{256... | collective-permute-start | bytes 43016 | tf_op jit(solution)/shard_map/ppermute | solution.py:14
  122.5 2.4 copy-start.1
  122.5 2.4 copy-start.2
  122.5 2.4 copy-start.3
  122.5 2.4 copy-start.6
  122.5 2.4 copy-start.7
  122.6 2.4 copy-start.8
  122.6 2.4 copy-start.9
  122.6 2.4 copy-start.10
  122.6 4.2 copy-start.4
  138.5 3.3 copy-start.13
Sparse Core Ops, SparseCore 0:
  141.9 310.5 all-reduce.2
where the time goes:
time: 464 us
  waiting for transfers between devices  312 us (67%)
  local copies, waits for them, and re-layouts  104 us (22%)
  other arithmetic  14.7 us (3%)
  between operations  14.1 us (3%)
  matrix products  9.63 us (2%)
  starting transfers between devices  9.13 us (2%)
    psum x1, waiting for transfers between devices, per_device(): everything = lax.psum(running, 'inst')  310 us
    gather x12, local copies, waits for them, and re-layouts, per_device(): neighbour = jnp.take(extended, face_nbr[direction], axis=2)  99.7 us
    dot_general x6, matrix products, face_jacobian(): jnp.einsum('imj,bmc->bijc', coupling, face_mean, precision=lax.Precision....  9.63 us
  transfers between devices with their start and end apart: 3, of which 2 were waited for; matrix products, arithmetic and copies ran while one was open for 1% of the time, Pallas kernels for 0%

commit v1 on v0

--- a/solution.py
+++ b/solution.py
@@ -77,7 +77,7 @@
         )
         face_mean, normal_flux = (face_mean, normal_flux)
         running = running + face_terms(face_mean, normal_flux, flux_left, flux_right)
-    everything = lax.psum(running, "inst")
+    everything = lax.all_gather(running, "inst").sum(axis=0)
     summed = lax.dynamic_slice_in_dim(
         everything, lax.axis_index("inst") * share_cells, share_cells, 2
     )

time: 464 us -> 361 us (0.78)
  the two profiles are of different devices: /device:TPU:2 before, /device:TPU:1 now
where the time goes in v1:
time: 361 us
  waiting for transfers between devices  203 us (56%)
  local copies, waits for them, and re-layouts  104 us (29%)
  other arithmetic  25.1 us (7%)
  between operations  14.1 us (4%)
  matrix products  9.65 us (3%)
  starting transfers between devices  5.26 us (1%)
    all_gather x1, waiting for transfers between devices, per_device(): everything = lax.all_gather(running, 'inst').sum(axis=0)  199 us
    gather x12, local copies, waits for them, and re-layouts, per_device(): neighbour = jnp.take(extended, face_nbr[direction], axis=2)  99.7 us
    reduce_sum x1, other arithmetic, per_device(): everything = lax.all_gather(running, 'inst').sum(axis=0)  10.9 us
    dot_general x6, matrix products, face_jacobian(): jnp.einsum('imj,bmc->bijc', coupling, face_mean, precision=lax.Precision....  9.65 us
  transfers between devices with their start and end apart: 3, of which 2 were waited for; matrix products, arithmetic and copies ran while one was open for 1% of the time, Pallas kernels for 0%

profile of v1, /device:TPU:1, one launch (start us, length us, event | category | flops | bytes accessed | tf_op | source)
XLA Modules:
  0.0 361.0 jit_solution(4329143518022592939)
XLA Ops:
  6.5 1.6 copy.196
  8.2 1.0 gather_fusion
  9.2 4.0 %collective-permute-start = (f32[1,7,512]{1,2,0:T(8,128)S(1)}, f32[1,7,512]{1,2,0:T(8,128)S(1)}, u32[]{:S(2)}, u32[]{:S(2)}) collective-permute-start(f32[1,7,512]{1,2,0:T(8,128)S(1)} %bitcast.358), channel_id=1, source_target_pairs={{0,32},{32,64},{64,96},{96,128},{128,160},{160,192},{192,224},{224... | collective-permute-start | bytes 43016 | tf_op jit(solution)/shard_map/ppermute | solution.py:14
  13.2 1.0 gather_fusion.1
  14.3 1.3 collective-permute-start.1
  15.6 0.1 fusion.97
  15.7 0.6 compare_and_fusion
  16.3 0.6 compare_and_fusion.2
  16.9 0.6 compare_and_fusion.4
  17.5 0.1 copy.199
  17.6 3.7 %collective-permute-done.1 = f32[1,7,512]{1,2,0:T(8,128)S(1)} collective-permute-done((f32[1,7,512]{1,2,0:T(8,128)S(1)}, f32[1,7,512]{1,2,0:T(8,128)S(1)}, u32[]{:S(2)}, u32[]{:S(2)}) %collective-permute-start.1) | collective-permute-done | bytes 14368 | tf_op jit(solution)/shard_map/ppermute | solution.py:14
  21.4 1.8 maximum_bitcast_fusion
  23.1 14.2 %gather_fusion.2 = f32[4096,7]{1,0:T(8,128)} fusion(f32[7,5120]{0,1:T(8,128)S(1)} %maximum_bitcast_fusion, s32[4096]{0:T(1024)S(1)} %fusion.74), kind=kCustom, calls=%fused_computation.clone | custom fusion | bytes 245760 | tf_op jit(solution)/shard_map/jit(_take)/gather | solution.py:70
  37.3 2.2 copy.197
  39.5 14.2 %gather_fusion.3 = f32[4096,7]{1,0:T(8,128)} fusion(f32[7,5120]{0,1:T(8,128)S(1)} %maximum_bitcast_fusion, s32[4096]{0:T(1024)S(1)} %fusion.75), kind=kCustom, calls=%fused_computation.1.clone | custom fusion | bytes 245760 | tf_op jit(solution)/shard_map/jit(_take)/gather | solution.py:70
  53.7 2.2 copy.200
  55.9 14.2 %gather_fusion.4 = f32[4096,7]{1,0:T(8,128)} fusion(f32[7,5120]{0,1:T(8,128)S(1)} %maximum_bitcast_fusion, s32[4096]{0:T(1024)S(1)} %fusion.76), kind=kCustom, calls=%fused_computation.2.clone | custom fusion | bytes 245760 | tf_op jit(solution)/shard_map/jit(_take)/gather | solution.py:70
  70.1 2.2 copy.202
  72.3 14.2 %gather_fusion.5 = f32[4096,7]{1,0:T(8,128)} fusion(f32[7,5120]{0,1:T(8,128)S(1)} %maximum_bitcast_fusion, s32[4096]{0:T(1024)S(1)} %fusion.77), kind=kCustom, calls=%fused_computation.3.clone | custom fusion | bytes 245760 | tf_op jit(solution)/shard_map/jit(_take)/gather | solution.py:70
  86.5 2.9 copy.204
  89.3 14.2 %gather_fusion.6 = f32[4096,7]{1,0:T(8,128)} fusion(f32[7,5120]{0,1:T(8,128)S(1)} %maximum_bitcast_fusion, s32[4096]{0:T(1024)S(1)} %fusion.78), kind=kCustom, calls=%fused_computation.4.clone | custom fusion | bytes 245760 | tf_op jit(solution)/shard_map/jit(_take)/gather | solution.py:70
  103.5 2.9 copy.206
  106.4 14.2 %gather_fusion.7 = f32[4096,7]{1,0:T(8,128)} fusion(f32[7,5120]{0,1:T(8,128)S(1)} %maximum_bitcast_fusion, s32[4096]{0:T(1024)S(1)} %fusion.79), kind=kCustom, calls=%fused_computation.5.clone | custom fusion | bytes 245760 | tf_op jit(solution)/shard_map/jit(_take)/gather | solution.py:70
  120.6 2.3 copy.208
  123.0 0.2 fusion.7
  123.2 1.7 fusion.36
  124.9 1.1 abs_reduce_fusion.5
  126.1 1.1 abs_reduce_fusion.4
  127.3 1.1 abs_reduce_fusion.3
  128.5 1.7 fusion.30
  130.2 2.1 abs_reduce_fusion.2
  132.3 2.1 abs_reduce_fusion.1
  134.5 2.1 abs_reduce_fusion
  136.6 3.4 add_multiply_fusion
  140.0 0.0 all-gather.2.cloned.1.call-update
  140.0 0.1 broadcast_multiply_fusion.1
  140.1 0.1 broadcast_multiply_fusion
  140.2 199.2 %all-gather.2.cloned.1.call-done = f32[32,7,7,4096]{3,2,1,0:T(8,128)} async-done(((f32[1,7,7,4096]{3,2,1,0:T(8,128)}), f32[32,7,7,4096]{3,2,1,0:T(8,128)}) %all-gather.2.cloned.1.call-update) | async-done | bytes 25690128 | tf_op jit(solution)/shard_map/all_gather | solution.py:80
  339.5 10.9 %reduce_sum.71 = f32[7,7,4096]{2,1,0:T(8,128)S(1)} reduce(f32[32,7,7,4096]{3,2,1,0:T(8,128)} %all-gather.2.cloned.1.call-done, f32[]{:T(128)} %constant.360.clone.1), dimensions={0}, to_apply=%region_12.14 | reduce | flops 6221824 | bytes 26492932 | tf_op jit(solution)/shard_map/reduce_sum | solution.py:80
  350.5 0.1 broadcast_in_dim.22
  350.7 0.2 fusion.6
  351.0 0.2 subtract_subtract_fusion.5
  351.4 0.2 subtract_subtract_fusion.4
  351.7 0.2 subtract_subtract_fusion.3
  352.1 0.2 subtract_subtract_fusion.2
  352.4 0.2 subtract_subtract_fusion.1
  352.8 0.2 subtract_subtract_fusion
  353.1 1.0 pad_maximum_fusion.1
  (95 shorter events, 1.1 us)
Async XLA Ops:
  6.5 1.6 copy-start.11
  6.5 9.0 %copy-start.5 = (s32[6,4096]{1,0:T(8,128)S(1)}, s32[6,4096]{1,0:T(8,128)}, u32[]{:S(2)}) copy-start(s32[6,4096]{1,0:T(8,128)} %param.38) | copy-start | bytes 294916
  6.5 11.0 %copy-start.12 = (f32[7,7]{1,0:T(8,128)S(1)}, f32[7,7]{1,0:T(8,128)}, u32[]{:S(2)}) copy-start(f32[7,7]{1,0:T(8,128)} %param.43) | copy-start | bytes 592
  6.5 332.9 %all-gather.2.cloned.1.call-start = ((), (), s32[]{:S(2)}) async-start(), calls=%async_computation | async-start | bytes 30277632 | tf_op jit(solution)/shard_map/all_gather | solution.py:80
  8.1 9.5 %copy-start = (f32[1,7,4096]{1,2,0:T(8,128)}, f32[1,7,4096]{1,2,0:T(8,128)S(1)}, u32[]{:S(2)}) copy-start(f32[1,7,4096]{1,2,0:T(8,128)S(1)} %copy.196) | copy-start | bytes 344068
  9.2 8.4 %collective-permute-start = (f32[1,7,512]{1,2,0:T(8,128)S(1)}, f32[1,7,512]{1,2,0:T(8,128)S(1)}, u32[]{:S(2)}, u32[]{:S(2)}) collective-permute-start(f32[1,7,512]{1,2,0:T(8,128)S(1)} %bitcast.358), channel_id=1, source_target_pairs={{0,32},{32,64},{64,96},{96,128},{128,160},{160,192},{192,224},{224... | collective-permute-start | bytes 43016 | tf_op jit(solution)/shard_map/ppermute | solution.py:14
  14.3 7.1 %collective-permute-start.1 = (f32[1,7,512]{1,2,0:T(8,128)S(1)}, f32[1,7,512]{1,2,0:T(8,128)S(1)}, u32[]{:S(2)}, u32[]{:S(2)}) collective-permute-start(f32[1,7,512]{1,2,0:T(8,128)S(1)} %bitcast.359), channel_id=1, source_target_pairs={{32,0},{64,32},{96,64},{128,96},{160,128},{192,160},{224,192},{256... | collective-permute-start | bytes 43016 | tf_op jit(solution)/shard_map/ppermute | solution.py:14
  120.5 2.4 copy-start.1
  120.5 2.4 copy-start.2
  120.5 2.4 copy-start.3
  120.5 2.4 copy-start.6
  120.6 2.4 copy-start.7
  120.6 2.4 copy-start.8
  120.6 2.4 copy-start.9
  120.6 2.4 copy-start.10
  120.6 4.3 %copy-start.4 = (f32[7,7]{1,0:T(8,128)S(1)}, f32[7,7]{1,0:T(8,128)}, u32[]{:S(2)}) copy-start(f32[7,7]{1,0:T(8,128)} %param.42) | copy-start | bytes 592
  136.6 3.4 copy-start.13
Sparse Core Ops, SparseCore 0:
  140.1 199.3 all-gather.1
